TPU v7x, 32 devices: a whole 2x2x4 slice. The times are simulated.
32 devices in a mesh: ctx: 16 (over z, y, core), fsdp: 2 (over x).
Axes of the slice: x: 2, y: 2, z: 4, core: 2. Of those that a mesh axis runs over, the one named last changes fastest.
Arguments:
- queries: bfloat16 [2, 2048, 2048], P('fsdp', 'ctx'), may hold values from -8 to 8
- keys_values: bfloat16 [2, 2048, 2, 2048], P('fsdp', 'ctx'), may hold values from -8 to 8
- upstream: bfloat16 [2, 2048, 2048], P('fsdp', 'ctx'), may hold values from -6 to 6
- out_weight: bfloat16 [2048, 2048], P('fsdp'), may hold values from -0.125 to 0.125
Outputs:
- grad_queries: bfloat16 [2, 2048, 2048], P('fsdp', 'ctx')
- grad_keys_values: bfloat16 [2, 2048, 2, 2048], P('fsdp', 'ctx')
- grad_weight: float32 [2048, 2048], P(('ctx', 'fsdp'))
All inputs are finite; a program needn't handle non-finite values.
Results may differ from a plain program's by a relative error of at most 0.014.
Values may be sent and summed in bfloat16 or wider, within the bound.
A program may use at most 128 MiB of HBM per device.

v0:
```python
import jax
import jax.numpy as jnp
from jax import lax
from jax.sharding import PartitionSpec as P

HEADS = 16
HEAD_DIM = 128
SPAN = 4
WINDOW = 512
NEGATIVE = -1e30


def passed_along(x, axis, by):
    count = lax.axis_size(axis)
    pairs = [(i, i + by) for i in range(count) if 0 <= i + by < count]
    return lax.ppermute(x, axis, pairs)


def shards(queries, keys_values, upstream, out_weight):
    seq_count, tok_rows, attn_width = queries.shape
    model_width = upstream.shape[2]
    head_count = HEADS
    head_size = HEAD_DIM
    reach_devices = SPAN
    inv_root = head_size ** (-0.5)
    flat_upstream = upstream.reshape(seq_count * tok_rows, model_width)
    grad_attn = jnp.dot(
        flat_upstream,
        lax.all_gather(out_weight, "fsdp", axis=0, tiled=True),
        preferred_element_type=jnp.float32,
    )
    grad_attn = grad_attn.astype(jnp.bfloat16).reshape(seq_count, tok_rows, head_count, head_size)
    moving = keys_values
    earlier = []
    for offset in range(reach_devices):
        moving = passed_along(moving, "ctx", 1)
        earlier = [moving] + earlier
    window_kv = jnp.concatenate(earlier + [keys_values], axis=1)
    key_count = window_kv.shape[1]
    key_heads = window_kv[:, :, 0].reshape(seq_count, key_count, head_count, head_size)
    value_heads = window_kv[:, :, 1].reshape(seq_count, key_count, head_count, head_size)
    query_heads = queries.reshape(seq_count, tok_rows, head_count, head_size)
    ctx_index = lax.axis_index("ctx")
    query_pos = ctx_index * tok_rows + jnp.arange(tok_rows, dtype=jnp.int32)
    key_pos = (ctx_index - reach_devices) * tok_rows + jnp.arange(key_count, dtype=jnp.int32)
    distance = query_pos[:, None] - key_pos[None, :]
    visible = (distance >= 0) & (distance < WINDOW) & (key_pos[None, :] >= 0)
    scores = (
        jnp.einsum("sqhe,skhe->shqk", query_heads, key_heads, preferred_element_type=jnp.float32)
        * inv_root
    )
    scores = jnp.where(visible[None, None], scores, NEGATIVE)
    row_max = jnp.max(scores, axis=-1, keepdims=True)
    lifted = jnp.exp(scores - row_max)
    probability = lifted / jnp.sum(lifted, axis=-1, keepdims=True)
    probs_low = probability.astype(jnp.bfloat16)
    attended = jnp.einsum(
        "shqk,skhe->sqhe", probs_low, value_heads, preferred_element_type=jnp.float32
    ).astype(jnp.bfloat16)
    products = jnp.einsum(
        "sqhe,skhe->shqk", grad_attn, value_heads, preferred_element_type=jnp.float32
    )
    center = jnp.sum(grad_attn.astype(jnp.float32) * attended.astype(jnp.float32), axis=-1)
    center = jnp.swapaxes(center, 1, 2)[:, :, :, None]
    grad_scores = (probability * (products - center)).astype(jnp.bfloat16)
    grad_queries = (
        jnp.einsum("shqk,skhe->sqhe", grad_scores, key_heads, preferred_element_type=jnp.float32)
        * inv_root
    )
    grad_queries = grad_queries.astype(jnp.bfloat16).reshape(seq_count, tok_rows, attn_width)
    grad_keys = (
        jnp.einsum("shqk,sqhe->skhe", grad_scores, query_heads, preferred_element_type=jnp.float32)
        * inv_root
    )
    grad_values = jnp.einsum(
        "shqk,sqhe->skhe", probs_low, grad_attn, preferred_element_type=jnp.float32
    )
    grad_window = jnp.stack(
        [
            grad_keys.reshape(seq_count, key_count, attn_width),
            grad_values.reshape(seq_count, key_count, attn_width),
        ],
        axis=2,
    )
    blocks = [
        grad_window[:, offset * tok_rows : (offset + 1) * tok_rows]
        for offset in range(reach_devices + 1)
    ]
    carried = blocks[0]
    for offset in range(1, reach_devices + 1):
        carried = passed_along(carried, "ctx", -1)
        if offset < reach_devices:
            carried = carried + blocks[offset]
    collected = blocks[reach_devices] + carried
    grad_pairs = collected.astype(jnp.bfloat16)
    flat_attended = attended.reshape(seq_count * tok_rows, attn_width)
    weight_term = lax.dot_general(
        flat_upstream, flat_attended, (((0,), (0,)), ((), ())), preferred_element_type=jnp.float32
    )
    weight_term = lax.optimization_barrier(weight_term.astype(jnp.bfloat16)).astype(jnp.float32)
    ctx_count = lax.axis_size("ctx")
    fsdp_count = lax.axis_size("fsdp")
    own_rows = model_width // (ctx_count * fsdp_count)
    weight_term = weight_term.reshape(ctx_count, fsdp_count, own_rows, attn_width)
    section_one = lax.psum_scatter(weight_term, "ctx", scatter_dimension=0, tiled=True)
    section_two = lax.psum_scatter(section_one, "fsdp", scatter_dimension=1, tiled=True)
    grad_weight = section_two.reshape(own_rows, attn_width)
    return (grad_queries, grad_pairs, grad_weight)


def solution(mesh):
    return jax.shard_map(
        shards,
        mesh=mesh,
        in_specs=(
            P("fsdp", "ctx", None),
            P("fsdp", "ctx", None, None),
            P("fsdp", "ctx", None),
            P("fsdp", None),
        ),
        out_specs=(P("fsdp", "ctx", None), P("fsdp", "ctx", None, None), P(("ctx", "fsdp"), None)),
        check_vma=False,
    )
```

profile of v0, /device:TPU:0, one launch (start us, length us, event | category | flops | bytes accessed | tf_op | source)
XLA Modules:
  0.0 428.0 jit_solution(18424261364848707581)
XLA Ops:
  8.0 2.5 copy.23
  10.5 2.5 collective-permute-start
  13.0 2.2 collective-permute-done
  15.2 14.0 %collective-permute-start.1 = (bf16[1,128,2,2048]{1,3,2,0:T(8,128)(2,1)S(1)}, bf16[1,128,2,2048]{1,3,2,0:T(8,128)(2,1)S(1)}, u32[]{:S(2)}, u32[]{:S(2)}) collective-permute-start(bf16[1,128,2,2048]{1,3,2,0:T(8,128)(2,1)S(1)} %collective-permute-done), channel_id=1, source_target_pairs={{0,2},{2,4},{4,6},{6,8},{8,10},{10,12},{12,14},{14,16},{16,18},{18... | collective-permute-start | bytes 3145736 | tf_op jit(solution)/shard_map/ppermute | solution.py:16
  29.2 2.2 collective-permute-done.1
  32.4 14.8 %collective-permute-start.2 = (bf16[1,128,2,2048]{1,3,2,0:T(8,128)(2,1)S(1)}, bf16[1,128,2,2048]{1,3,2,0:T(8,128)(2,1)}, u32[]{:S(2)}, u32[]{:S(2)}) collective-permute-start(bf16[1,128,2,2048]{1,3,2,0:T(8,128)(2,1)S(1)} %collective-permute-done.1), channel_id=1, source_target_pairs={{0,2},{2,4},{4,6},{6,8},{8,10},{10,12},{12,14},{14,16},{16,18},{18... | collective-permute-start | bytes 3145736 | tf_op jit(solution)/shard_map/ppermute | solution.py:16
  48.7 14.7 %collective-permute-start.3 = (bf16[1,128,2,2048]{1,3,2,0:T(8,128)(2,1)}, bf16[1,128,2,2048]{1,3,2,0:T(8,128)(2,1)}, u32[]{:S(2)}, u32[]{:S(2)}) collective-permute-start(bf16[1,128,2,2048]{1,3,2,0:T(8,128)(2,1)} %collective-permute-done.2), channel_id=1, source_target_pairs={{0,2},{2,4},{4,6},{6,8},{8,10},{10,12},{12,14},{14,16},{16,18},{18... | collective-permute-start | bytes 3145736 | tf_op jit(solution)/shard_map/ppermute | solution.py:16
  67.9 1.5 constant_dynamic-update-slice_fusion.2
  69.9 2.0 fusion.24
  71.8 5.8 %fusion.25 = (f32[16,128]{1,0:T(8,128)S(1)}, f32[16,128,640]{1,2,0:T(8,128)}) fusion(pred[128,640]{0,1:T(8,128)(4,1)S(1)} %fusion.19, bf16[640,16,128]{0,2,1:T(8,128)(2,1)S(1)} %bitcast.80, bf16[128,16,128]{0,2,1:T(8,128)(2,1)} %bitcast.86), kind=kOutput, calls=%fused_computation.53 | convolution fusion | flops 340787840 | bytes 8478720 | tf_op jit(solution)/shard_map/sub | solution.py:54
  77.6 3.1 fusion.5
  80.8 35.5 %all-gather.2.cloned.1.call-done = bf16[2048,2048]{1,0:T(8,128)(2,1)} async-done(((bf16[1024,2048]{1,0:T(8,128)(2,1)}), bf16[2048,2048]{1,0:T(8,128)(2,1)}) %all-gather.2.cloned.1.call-update) | async-done | bytes 8388624 | tf_op jit(solution)/shard_map/all_gather | solution.py:29
  116.3 5.5 %convolution_convert_fusion = bf16[128,2048]{1,0:T(8,128)(2,1)} fusion(bf16[2048,2048]{1,0:T(8,128)(2,1)} %all-gather.2.cloned.1.call-done, bf16[1,128,2048]{2,1,0:T(8,128)(2,1)S(1)} %copy-done), kind=kOutput, calls=%fused_computation.19 | convolution fusion | flops 1074003968 | bytes 9437184 | tf_op jit(solution)/shard_map/dot_general | solution.py:27
  121.8 2.2 copy.50
  124.0 2.9 multiply_reduce_fusion
  126.8 5.6 %convert_bitcast_fusion = bf16[2048,2048]{0,1:T(8,128)(2,1)} fusion(bf16[128,2048]{0,1:T(8,128)(2,1)S(1)} %bitcast.85, bf16[1,128,2048]{2,1,0:T(8,128)(2,1)S(1)} %copy-done), kind=kOutput, calls=%fused_computation.9 | convolution fusion | flops 1077936128 | bytes 9437184 | tf_op jit(solution)/shard_map/dot_general | solution.py:97
  132.5 13.0 %copy.39 = f32[2048,2048]{1,0:T(8,128)} copy(bf16[2048,2048]{0,1:T(8,128)(2,1)} %convert_bitcast_fusion) | data formatting | bytes 25165824 | tf_op jit(solution)/shard_map/reshape | solution.py:104
  147.5 4.8 %multiply_convert_fusion = bf16[16,128,640]{1,2,0:T(8,128)(2,1)S(1)} fusion(f32[16,128]{1,0:T(8,128)S(1)} %bitcast.91, bf16[128,16,128]{0,2,1:T(8,128)(2,1)} %bitcast.88, bf16[640,16,128]{0,2,1:T(8,128)(2,1)} %bitcast.83, f32[16,128,640]{1,2,0:T(8,128)} %get-tuple-element.12, f32[16,128]{1,0:T(8,128)S(1)} %get-tuple-element.11), kind=kOutput, calls=%fused_computation.12 | convolution fusion | flops 340787200 | bytes 11026432 | tf_op jit(solution)/shard_map/sqhe,skhe->shqk/dot_general | solution.py:60
  153.8 3.7 multiply_bitcast_fusion
  157.5 6.7 %copy.36 = f32[1,640,16,128]{1,3,2,0:T(8,128)} copy(f32[1,640,16,128]{3,1,2,0:T(8,128)} %multiply_bitcast_fusion) | data formatting | bytes 10485760 | tf_op jit(solution)/shard_map/mul | solution.py:72
  165.2 4.2 copy-done.2
  170.9 4.8 %collective-permute-done.4 = f32[1,128,2,2048]{1,3,2,0:T(8,128)S(1)} collective-permute-done((f32[1,128,2,2048]{1,3,2,0:T(8,128)S(1)}, f32[1,128,2,2048]{1,3,2,0:T(8,128)S(1)}, u32[]{:S(2)}, u32[]{:S(2)}) %collective-permute-start.4) | collective-permute-done | bytes 2097184 | tf_op jit(solution)/shard_map/ppermute | solution.py:16
  177.3 36.9 %collective-permute-done.5 = f32[1,128,2,2048]{1,3,2,0:T(8,128)S(1)} collective-permute-done((f32[1,128,2,2048]{1,3,2,0:T(8,128)S(1)}, f32[1,128,2,2048]{1,3,2,0:T(8,128)S(1)}, u32[]{:S(2)}, u32[]{:S(2)}) %collective-permute-start.5) | collective-permute-done | bytes 2097184 | tf_op jit(solution)/shard_map/ppermute | solution.py:16
  214.5 1.6 collective-permute-start.6
  216.1 37.7 %collective-permute-done.6 = f32[1,128,2,2048]{1,3,2,0:T(8,128)S(1)} collective-permute-done((f32[1,128,2,2048]{1,3,2,0:T(8,128)S(1)}, f32[1,128,2,2048]{1,3,2,0:T(8,128)S(1)}, u32[]{:S(2)}, u32[]{:S(2)}) %collective-permute-start.6) | collective-permute-done | bytes 2097184 | tf_op jit(solution)/shard_map/ppermute | solution.py:16
  253.8 1.6 fusion.14
  256.6 142.5 %reduce-scatter.3.cloned.1.call-done = f32[1,2,64,2048]{3,2,1,0:T(8,128)} async-done(((f32[16,2,64,2048]{3,2,1,0:T(8,128)}), f32[1,2,64,2048]{3,2,1,0:T(8,128)}) %reduce-scatter.3.cloned.1.call-update) | async-done | bytes 1048592 | tf_op jit(solution)/shard_map/reduce_scatter | solution.py:105
  399.2 3.4 fusion.15
  402.6 2.1 copy.40
  404.7 2.4 fusion.10
  407.1 2.0 copy.41
  409.1 12.4 %reduce-scatter.5.cloned.1.call-done = f32[1,1,64,2048]{3,2,1,0:T(8,128)} async-done(((f32[1,2,64,2048]{3,2,1,0:T(8,128)}), f32[1,1,64,2048]{3,2,1,0:T(8,128)}) %reduce-scatter.5.cloned.1.call-update) | async-done | bytes 524304 | tf_op jit(solution)/shard_map/reduce_scatter | solution.py:106
  (49 shorter events, 17.3 us)
Async XLA Ops:
  7.2 109.1 %copy-start = (bf16[1,128,2048]{2,1,0:T(8,128)(2,1)S(1)}, bf16[1,128,2048]{2,1,0:T(8,128)(2,1)}, u32[]{:S(2)}) copy-start(bf16[1,128,2048]{2,1,0:T(8,128)(2,1)} %param.6) | copy-start | bytes 1572868
  7.2 56.2 %copy-start.11 = (bf16[1,128,2048]{2,1,0:T(8,128)(2,1)S(1)}, bf16[1,128,2048]{2,1,0:T(8,128)(2,1)}, u32[]{:S(2)}) copy-start(bf16[1,128,2048]{2,1,0:T(8,128)(2,1)} %param.4) | copy-start | bytes 1572868
  7.2 109.1 %all-gather.2.cloned.1.call-start = ((), (), s32[]{:S(2)}) async-start(), calls=%async_computation.2 | async-start | bytes 12582912 | tf_op jit(solution)/shard_map/all_gather | solution.py:29
  7.9 391.2 %reduce-scatter.3.cloned.1.call-start = ((), (), s32[]{:S(2)}) async-start(), calls=%async_computation.3 | async-start | bytes 17825792 | tf_op jit(solution)/shard_map/reduce_scatter | solution.py:105
  10.5 4.7 %collective-permute-start = (bf16[1,128,2,2048]{1,3,2,0:T(8,128)(2,1)S(1)}, bf16[1,128,2,2048]{1,3,2,0:T(8,128)(2,1)S(1)}, u32[]{:S(2)}, u32[]{:S(2)}) collective-permute-start(bf16[1,128,2,2048]{1,3,2,0:T(8,128)(2,1)S(1)} %copy.23), channel_id=1, source_target_pairs={{0,2},{2,4},{4,6},{6,8},{8,10},{10,12},{12,14},{14,16},{16,18},{18... | collective-permute-start | bytes 3145736 | tf_op jit(solution)/shard_map/ppermute | solution.py:16
  15.2 16.2 %collective-permute-start.1 = (bf16[1,128,2,2048]{1,3,2,0:T(8,128)(2,1)S(1)}, bf16[1,128,2,2048]{1,3,2,0:T(8,128)(2,1)S(1)}, u32[]{:S(2)}, u32[]{:S(2)}) collective-permute-start(bf16[1,128,2,2048]{1,3,2,0:T(8,128)(2,1)S(1)} %collective-permute-done), channel_id=1, source_target_pairs={{0,2},{2,4},{4,6},{6,8},{8,10},{10,12},{12,14},{14,16},{16,18},{18... | collective-permute-start | bytes 3145736 | tf_op jit(solution)/shard_map/ppermute | solution.py:16
  31.4 1.0 copy-start.10
  32.4 16.2 %collective-permute-start.2 = (bf16[1,128,2,2048]{1,3,2,0:T(8,128)(2,1)S(1)}, bf16[1,128,2,2048]{1,3,2,0:T(8,128)(2,1)}, u32[]{:S(2)}, u32[]{:S(2)}) collective-permute-start(bf16[1,128,2,2048]{1,3,2,0:T(8,128)(2,1)S(1)} %collective-permute-done.1), channel_id=1, source_target_pairs={{0,2},{2,4},{4,6},{6,8},{8,10},{10,12},{12,14},{14,16},{16,18},{18... | collective-permute-start | bytes 3145736 | tf_op jit(solution)/shard_map/ppermute | solution.py:16
  48.7 16.3 %collective-permute-start.3 = (bf16[1,128,2,2048]{1,3,2,0:T(8,128)(2,1)}, bf16[1,128,2,2048]{1,3,2,0:T(8,128)(2,1)}, u32[]{:S(2)}, u32[]{:S(2)}) collective-permute-start(bf16[1,128,2,2048]{1,3,2,0:T(8,128)(2,1)} %collective-permute-done.2), channel_id=1, source_target_pairs={{0,2},{2,4},{4,6},{6,8},{8,10},{10,12},{12,14},{14,16},{16,18},{18... | collective-permute-start | bytes 3145736 | tf_op jit(solution)/shard_map/ppermute | solution.py:16
  71.8 5.8 %copy-start.4 = (bf16[1,640,1,2048]{1,3,2,0:T(8,128)(2,1)}, bf16[1,640,1,2048]{1,3,2,0:T(8,128)(2,1)S(1)}, u32[]{:S(2)}) copy-start(bf16[1,640,1,2048]{1,3,2,0:T(8,128)(2,1)S(1)} %get-tuple-element.10) | copy-start | bytes 7864324
  145.5 1.0 copy-start.7
  145.5 276.0 %reduce-scatter.5.cloned.1.call-start = ((), (), s32[]{:S(2)}) async-start(), calls=%async_computation.4 | async-start | bytes 1572864 | tf_op jit(solution)/shard_map/reduce_scatter | solution.py:106
  147.5 6.3 %copy-start.8 = (bf16[1,128,2048]{1,2,0:T(8,128)(2,1)S(1)}, bf16[1,128,2048]{1,2,0:T(8,128)(2,1)}, u32[]{:S(2)}) copy-start(bf16[1,128,2048]{1,2,0:T(8,128)(2,1)} %copy.51) | copy-start | bytes 1572868
  152.3 1.5 copy-start.6
  157.5 6.7 %copy-start.9 = (bf16[128,2048]{0,1:T(8,128)(2,1)S(1)}, bf16[128,2048]{0,1:T(8,128)(2,1)}, u32[]{:S(2)}) copy-start(bf16[128,2048]{0,1:T(8,128)(2,1)} %copy.52) | copy-start | bytes 1572868
  164.2 5.3 %copy-start.2 = (f32[1,640,16,128]{1,3,2,0:T(8,128)S(1)}, f32[1,640,16,128]{1,3,2,0:T(8,128)}, u32[]{:S(2)}) copy-start(f32[1,640,16,128]{1,3,2,0:T(8,128)} %copy.36) | copy-start | bytes 15728644
  165.2 88.5 %copy-start.3 = (f32[16,128,640]{2,1,0:T(8,128)}, f32[16,128,640]{2,1,0:T(8,128)S(1)}, u32[]{:S(2)}) copy-start(f32[16,128,640]{2,1,0:T(8,128)S(1)} %fusion.26) | copy-start | bytes 15728644
  169.6 6.1 %collective-permute-start.4 = (f32[1,128,2,2048]{1,3,2,0:T(8,128)S(1)}, f32[1,128,2,2048]{1,3,2,0:T(8,128)S(1)}, u32[]{:S(2)}, u32[]{:S(2)}) collective-permute-start(f32[1,128,2,2048]{1,3,2,0:T(8,128)S(1)} %fusion.11), channel_id=1, source_target_pairs={{2,0},{4,2},{6,4},{8,6},{10,8},{12,10},{14,12},{16,14},{18,16},{20... | collective-permute-start | bytes 6291464 | tf_op jit(solution)/shard_map/ppermute | solution.py:16
  176.1 38.2 %collective-permute-start.5 = (f32[1,128,2,2048]{1,3,2,0:T(8,128)S(1)}, f32[1,128,2,2048]{1,3,2,0:T(8,128)S(1)}, u32[]{:S(2)}, u32[]{:S(2)}) collective-permute-start(f32[1,128,2,2048]{1,3,2,0:T(8,128)S(1)} %fusion.13), channel_id=1, source_target_pairs={{2,0},{4,2},{6,4},{8,6},{10,8},{12,10},{14,12},{16,14},{18,16},{20... | collective-permute-start | bytes 6291464 | tf_op jit(solution)/shard_map/ppermute | solution.py:16
  214.5 184.7 %copy-start.5 = (bf16[1,640,1,2048]{1,3,2,0:T(8,128)(2,1)S(1)}, bf16[1,640,1,2048]{1,3,2,0:T(8,128)(2,1)}, u32[]{:S(2)}) copy-start(bf16[1,640,1,2048]{1,3,2,0:T(8,128)(2,1)} %copy-done.4) | copy-start | bytes 7864324
  214.5 39.3 %collective-permute-start.6 = (f32[1,128,2,2048]{1,3,2,0:T(8,128)S(1)}, f32[1,128,2,2048]{1,3,2,0:T(8,128)S(1)}, u32[]{:S(2)}, u32[]{:S(2)}) collective-permute-start(f32[1,128,2,2048]{1,3,2,0:T(8,128)S(1)} %fusion.7), channel_id=1, source_target_pairs={{2,0},{4,2},{6,4},{8,6},{10,8},{12,10},{14,12},{16,14},{18,16},{20... | collective-permute-start | bytes 6291464 | tf_op jit(solution)/shard_map/ppermute | solution.py:16
  255.4 149.3 %collective-permute-start.7 = (f32[1,128,2,2048]{1,3,2,0:T(8,128)}, f32[1,128,2,2048]{1,3,2,0:T(8,128)}, u32[]{:S(2)}, u32[]{:S(2)}) collective-permute-start(f32[1,128,2,2048]{1,3,2,0:T(8,128)} %fusion.14), channel_id=1, source_target_pairs={{2,0},{4,2},{6,4},{8,6},{10,8},{12,10},{14,12},{16,14},{18,16},{20... | collective-permute-start | bytes 6291464 | tf_op jit(solution)/shard_map/ppermute | solution.py:16
  402.6 18.9 %copy-start.1 = (bf16[1,128,2048]{2,1,0:T(8,128)(2,1)S(1)}, bf16[1,128,2048]{2,1,0:T(8,128)(2,1)}, u32[]{:S(2)}) copy-start(bf16[1,128,2048]{2,1,0:T(8,128)(2,1)} %param.6) | copy-start | bytes 1572868
Sparse Core Ops, SparseCore 0:
  9.5 106.6 all-gather.1
  145.6 253.4 reduce-scatter.2
  402.0 19.4 reduce-scatter.4
where the time goes:
time: 429 us; the launch traced here: 428 us
  waiting for transfers between devices  277 us (65%)
  starting transfers between devices  51.7 us (12%)
  local copies, waits for them, and re-layouts  44.9 us (10%)
  matrix products  32.7 us (8%)
  between operations  13.9 us (3%)
  other arithmetic  8.09 us (2%)
    reduce_scatter x1, waiting for transfers between devices, shards(): lax.psum_scatter(weight_term, 'ctx', scatter_dimension=0, tiled=True)  143 us
    ppermute x8, waiting for transfers between devices, passed_along(): return lax.ppermute(x, axis, pairs)  85.5 us
    ppermute x8, starting transfers between devices, passed_along(): return lax.ppermute(x, axis, pairs)  51.4 us
    all_gather x1, waiting for transfers between devices, shards(): lax.all_gather(out_weight, 'fsdp', axis=0, tiled=True)  35.5 us
    unnamed x31, local copies, waits for them, and re-layouts  18.8 us
    reshape x1, local copies, waits for them, and re-layouts, shards(): weight_term.reshape(ctx_count, fsdp_count, own_rows, attn_width)  13 us
    reduce_scatter x1, waiting for transfers between devices, shards(): lax.psum_scatter(section_one, 'fsdp', scatter_dimension=1, tiled=True)  12.4 us
  transfers between devices with their start and end apart: 11, of which 10 were waited for; matrix products, arithmetic and copies ran while one was open for 11% of the time, Pallas kernels for 0%

commit v1 on v0

--- a/solution.py
+++ b/solution.py
@@ -1,3 +1,4 @@
+import functools
 import jax
 import jax.numpy as jnp
 from jax import lax
@@ -8,6 +9,23 @@
 SPAN = 4
 WINDOW = 512
 NEGATIVE = -1e30
+
+
+def manage_run(vec, in_dim):
+    spare = lax.psum(1, "fsdp")
+    all_rows = lax.axis_index("fsdp")
+    w1, z, local_part = (spare, all_rows, vec.shape[in_dim])
+    taken_in, reply = (vec, 1)
+    while reply < w1:
+        slots = []
+        for dev_i in range(w1):
+            slots.append((dev_i, (dev_i - reply) % w1))
+        taken_in = jnp.concatenate([taken_in, lax.ppermute(taken_in, "fsdp", slots)], axis=in_dim)
+        reply = 2 * reply
+    return jnp.roll(taken_in, z * local_part, in_dim)
+
+
+region_proceed = functools.partial(manage_run, in_dim=0)
 
 
 def passed_along(x, axis, by):
@@ -25,9 +43,7 @@
     inv_root = head_size ** (-0.5)
     flat_upstream = upstream.reshape(seq_count * tok_rows, model_width)
     grad_attn = jnp.dot(
-        flat_upstream,
-        lax.all_gather(out_weight, "fsdp", axis=0, tiled=True),
-        preferred_element_type=jnp.float32,
+        flat_upstream, region_proceed(out_weight), preferred_element_type=jnp.float32
     )
     grad_attn = grad_attn.astype(jnp.bfloat16).reshape(seq_count, tok_rows, head_count, head_size)
     moving = keys_values

time: 429 us -> 399 us (0.930)
  the two profiles are of different devices: /device:TPU:0 before, /device:TPU:5 now
where the time goes in v1:
time: 399 us; the launch traced here: 398 us
  waiting for transfers between devices  270 us (68%)
  local copies, waits for them, and re-layouts  40.7 us (10%)
  matrix products  35.8 us (9%)
  starting transfers between devices  29.1 us (7%)
  between operations  14.3 us (4%)
  other arithmetic  8.39 us (2%)
    ppermute x8, waiting for transfers between devices, passed_along(): return lax.ppermute(x, axis, pairs)  179 us
    ppermute x1, waiting for transfers between devices, manage_run(): lax.ppermute(taken_in, 'fsdp', slots)  90.8 us
    ppermute x8, starting transfers between devices, passed_along(): return lax.ppermute(x, axis, pairs)  27.6 us
    unnamed x37, local copies, waits for them, and re-layouts  17.4 us
    reshape x1, local copies, waits for them, and re-layouts, shards(): weight_term.reshape(ctx_count, fsdp_count, own_rows, attn_width)  13 us
    dot_general x1, matrix products, shards(): jnp.dot(flat_upstream, region_proceed(out_weight), preferred_element_type...  11.9 us
  transfers between devices with their start and end apart: 11, of which 9 were waited for; matrix products, arithmetic and copies ran while one was open for 10% of the time, Pallas kernels for 0%

profile of v1, /device:TPU:5, one launch (start us, length us, event | category | flops | bytes accessed | tf_op | source)
XLA Modules:
  0.0 398.0 jit_solution(14290053242129361835)
XLA Ops:
  7.2 2.6 copy.21
  9.8 3.7 collective-permute-start
  13.5 11.7 %collective-permute-done = bf16[1,128,2,2048]{1,3,2,0:T(8,128)(2,1)S(1)} collective-permute-done((bf16[1,128,2,2048]{1,3,2,0:T(8,128)(2,1)S(1)}, bf16[1,128,2,2048]{1,3,2,0:T(8,128)(2,1)S(1)}, u32[]{:S(2)}, u32[]{:S(2)}) %collective-permute-start) | collective-permute-done | bytes 1048608 | tf_op jit(solution)/shard_map/ppermute | solution.py:34
  25.3 5.3 %collective-permute-start.1 = (bf16[1,128,2,2048]{1,3,2,0:T(8,128)(2,1)S(1)}, bf16[1,128,2,2048]{1,3,2,0:T(8,128)(2,1)S(1)}, u32[]{:S(2)}, u32[]{:S(2)}) collective-permute-start(bf16[1,128,2,2048]{1,3,2,0:T(8,128)(2,1)S(1)} %collective-permute-done), channel_id=1, source_target_pairs={{0,2},{2,4},{4,6},{6,8},{8,10},{10,12},{12,14},{14,16},{16,18},{18... | collective-permute-start | bytes 3145736 | tf_op jit(solution)/shard_map/ppermute | solution.py:34
  30.6 11.7 %collective-permute-done.1 = bf16[1,128,2,2048]{1,3,2,0:T(8,128)(2,1)S(1)} collective-permute-done((bf16[1,128,2,2048]{1,3,2,0:T(8,128)(2,1)S(1)}, bf16[1,128,2,2048]{1,3,2,0:T(8,128)(2,1)S(1)}, u32[]{:S(2)}, u32[]{:S(2)}) %collective-permute-start.1) | collective-permute-done | bytes 1048608 | tf_op jit(solution)/shard_map/ppermute | solution.py:34
  43.2 5.3 %collective-permute-start.2 = (bf16[1,128,2,2048]{1,3,2,0:T(8,128)(2,1)S(1)}, bf16[1,128,2,2048]{1,3,2,0:T(8,128)(2,1)}, u32[]{:S(2)}, u32[]{:S(2)}) collective-permute-start(bf16[1,128,2,2048]{1,3,2,0:T(8,128)(2,1)S(1)} %collective-permute-done.1), channel_id=1, source_target_pairs={{0,2},{2,4},{4,6},{6,8},{8,10},{10,12},{12,14},{14,16},{16,18},{18... | collective-permute-start | bytes 3145736 | tf_op jit(solution)/shard_map/ppermute | solution.py:34
  48.5 11.7 %collective-permute-done.2 = bf16[1,128,2,2048]{1,3,2,0:T(8,128)(2,1)} collective-permute-done((bf16[1,128,2,2048]{1,3,2,0:T(8,128)(2,1)S(1)}, bf16[1,128,2,2048]{1,3,2,0:T(8,128)(2,1)}, u32[]{:S(2)}, u32[]{:S(2)}) %collective-permute-start.2) | collective-permute-done | bytes 1048608 | tf_op jit(solution)/shard_map/ppermute | solution.py:34
  60.3 5.4 %collective-permute-start.3 = (bf16[1,128,2,2048]{1,3,2,0:T(8,128)(2,1)}, bf16[1,128,2,2048]{1,3,2,0:T(8,128)(2,1)}, u32[]{:S(2)}, u32[]{:S(2)}) collective-permute-start(bf16[1,128,2,2048]{1,3,2,0:T(8,128)(2,1)} %collective-permute-done.2), channel_id=1, source_target_pairs={{0,2},{2,4},{4,6},{6,8},{8,10},{10,12},{12,14},{14,16},{16,18},{18... | collective-permute-start | bytes 3145736 | tf_op jit(solution)/shard_map/ppermute | solution.py:34
  65.6 2.0 copy.47
  68.0 9.7 %collective-permute-done.3 = bf16[1,128,2,2048]{1,3,2,0:T(8,128)(2,1)} collective-permute-done((bf16[1,128,2,2048]{1,3,2,0:T(8,128)(2,1)}, bf16[1,128,2,2048]{1,3,2,0:T(8,128)(2,1)}, u32[]{:S(2)}, u32[]{:S(2)}) %collective-permute-start.3) | collective-permute-done | bytes 1048608 | tf_op jit(solution)/shard_map/ppermute | solution.py:34
  82.6 2.0 fusion.35
  84.5 5.8 %fusion.36 = (f32[16,128]{1,0:T(8,128)S(1)}, f32[16,128,640]{1,2,0:T(8,128)}) fusion(pred[128,640]{0,1:T(8,128)(4,1)S(1)} %fusion.28, bf16[640,16,128]{0,2,1:T(8,128)(2,1)S(1)} %bitcast.83, bf16[128,16,128]{0,2,1:T(8,128)(2,1)} %bitcast.88), kind=kOutput, calls=%fused_computation.64 | convolution fusion | flops 340787840 | bytes 8478720 | tf_op jit(solution)/shard_map/sub | solution.py:70
  90.3 3.3 fusion.13
  95.3 5.6 %convert_bitcast_fusion = bf16[2048,2048]{0,1:T(8,128)(2,1)} fusion(bf16[128,2048]{0,1:T(8,128)(2,1)S(1)} %bitcast.87, bf16[1,128,2048]{2,1,0:T(8,128)(2,1)S(1)} %copy-done), kind=kOutput, calls=%fused_computation.16 | convolution fusion | flops 1077936128 | bytes 9437184 | tf_op jit(solution)/shard_map/dot_general | solution.py:113
  100.9 13.0 %copy.35 = f32[2048,2048]{1,0:T(8,128)} copy(bf16[2048,2048]{0,1:T(8,128)(2,1)} %convert_bitcast_fusion) | data formatting | bytes 25165824 | tf_op jit(solution)/shard_map/reshape | solution.py:120
  115.5 90.8 %collective-permute-done.4 = bf16[1024,2048]{1,0:T(8,128)(2,1)} collective-permute-done((bf16[1024,2048]{1,0:T(8,128)(2,1)}, bf16[1024,2048]{1,0:T(8,128)(2,1)}, u32[]{:S(2)}, u32[]{:S(2)}) %collective-permute-start.4) | collective-permute-done | bytes 4194336 | tf_op jit(solution)/shard_map/ppermute | solution.py:23
  206.3 11.9 %fusion.10 = bf16[2048,128]{1,0:T(8,128)(2,1)S(1)} fusion(s32[]{:T(128)S(6)} %select_n.20, bf16[1024,2048]{1,0:T(8,128)(2,1)} %param.7, bf16[1024,2048]{1,0:T(8,128)(2,1)} %collective-permute-done.4, bf16[1,128,2048]{2,1,0:T(8,128)(2,1)S(1)} %copy-done), kind=kOutput, calls=%fused_computation.27 | convolution fusion | flops 1107558400 | bytes 9437188 | tf_op jit(solution)/shard_map/dot_general | solution.py:45
  218.5 4.0 multiply_convert_fusion
  223.9 3.1 multiply_bitcast_fusion
  227.1 6.1 %copy.33 = f32[1,640,16,128]{1,3,2,0:T(8,128)} copy(f32[1,640,16,128]{3,1,2,0:T(8,128)} %multiply_bitcast_fusion) | data formatting | bytes 10485760 | tf_op jit(solution)/shard_map/mul | solution.py:88
  234.2 2.8 copy-done.2
  237.1 1.9 collective-permute-start.5
  239.1 26.4 %collective-permute-done.5 = f32[1,128,2,2048]{1,3,2,0:T(8,128)S(1)} collective-permute-done((f32[1,128,2,2048]{1,3,2,0:T(8,128)S(1)}, f32[1,128,2,2048]{1,3,2,0:T(8,128)S(1)}, u32[]{:S(2)}, u32[]{:S(2)}) %collective-permute-start.5) | collective-permute-done | bytes 2097184 | tf_op jit(solution)/shard_map/ppermute | solution.py:34
  265.9 1.9 collective-permute-start.6
  267.8 60.0 %collective-permute-done.6 = f32[1,128,2,2048]{1,3,2,0:T(8,128)S(1)} collective-permute-done((f32[1,128,2,2048]{1,3,2,0:T(8,128)S(1)}, f32[1,128,2,2048]{1,3,2,0:T(8,128)S(1)}, u32[]{:S(2)}, u32[]{:S(2)}) %collective-permute-start.6) | collective-permute-done | bytes 2097184 | tf_op jit(solution)/shard_map/ppermute | solution.py:34
  328.0 2.2 collective-permute-start.7
  330.2 26.3 %collective-permute-done.7 = f32[1,128,2,2048]{1,3,2,0:T(8,128)S(1)} collective-permute-done((f32[1,128,2,2048]{1,3,2,0:T(8,128)S(1)}, f32[1,128,2,2048]{1,3,2,0:T(8,128)S(1)}, u32[]{:S(2)}, u32[]{:S(2)}) %collective-permute-start.7) | collective-permute-done | bytes 2097184 | tf_op jit(solution)/shard_map/ppermute | solution.py:34
  360.1 3.4 fusion.23
  363.5 2.1 copy.36
  365.6 21.1 %collective-permute-done.8 = f32[1,128,2,2048]{1,3,2,0:T(8,128)} collective-permute-done((f32[1,128,2,2048]{1,3,2,0:T(8,128)}, f32[1,128,2,2048]{1,3,2,0:T(8,128)}, u32[]{:S(2)}, u32[]{:S(2)}) %collective-permute-start.8) | collective-permute-done | bytes 2097184 | tf_op jit(solution)/shard_map/ppermute | solution.py:34
  386.7 2.4 fusion.18
  389.1 2.0 copy.37
  (53 shorter events, 16.3 us)
Async XLA Ops:
  7.2 88.2 %copy-start = (bf16[1,128,2048]{2,1,0:T(8,128)(2,1)S(1)}, bf16[1,128,2048]{2,1,0:T(8,128)(2,1)}, u32[]{:S(2)}) copy-start(bf16[1,128,2048]{2,1,0:T(8,128)(2,1)} %param.6) | copy-start | bytes 1572868
  7.2 352.9 %reduce-scatter.3.cloned.1.call-start = ((), (), s32[]{:S(2)}) async-start(), calls=%async_computation.2 | async-start | bytes 17825792 | tf_op jit(solution)/shard_map/reduce_scatter | solution.py:121
  9.8 15.4 %collective-permute-start = (bf16[1,128,2,2048]{1,3,2,0:T(8,128)(2,1)S(1)}, bf16[1,128,2,2048]{1,3,2,0:T(8,128)(2,1)S(1)}, u32[]{:S(2)}, u32[]{:S(2)}) collective-permute-start(bf16[1,128,2,2048]{1,3,2,0:T(8,128)(2,1)S(1)} %copy.21), channel_id=1, source_target_pairs={{0,2},{2,4},{4,6},{6,8},{8,10},{10,12},{12,14},{14,16},{16,18},{18... | collective-permute-start | bytes 3145736 | tf_op jit(solution)/shard_map/ppermute | solution.py:34
  25.3 17.0 %collective-permute-start.1 = (bf16[1,128,2,2048]{1,3,2,0:T(8,128)(2,1)S(1)}, bf16[1,128,2,2048]{1,3,2,0:T(8,128)(2,1)S(1)}, u32[]{:S(2)}, u32[]{:S(2)}) collective-permute-start(bf16[1,128,2,2048]{1,3,2,0:T(8,128)(2,1)S(1)} %collective-permute-done), channel_id=1, source_target_pairs={{0,2},{2,4},{4,6},{6,8},{8,10},{10,12},{12,14},{14,16},{16,18},{18... | collective-permute-start | bytes 3145736 | tf_op jit(solution)/shard_map/ppermute | solution.py:34
  42.3 1.0 copy-start.14
  43.2 17.0 %collective-permute-start.2 = (bf16[1,128,2,2048]{1,3,2,0:T(8,128)(2,1)S(1)}, bf16[1,128,2,2048]{1,3,2,0:T(8,128)(2,1)}, u32[]{:S(2)}, u32[]{:S(2)}) collective-permute-start(bf16[1,128,2,2048]{1,3,2,0:T(8,128)(2,1)S(1)} %collective-permute-done.1), channel_id=1, source_target_pairs={{0,2},{2,4},{4,6},{6,8},{8,10},{10,12},{12,14},{14,16},{16,18},{18... | collective-permute-start | bytes 3145736 | tf_op jit(solution)/shard_map/ppermute | solution.py:34
  60.3 17.4 %collective-permute-start.3 = (bf16[1,128,2,2048]{1,3,2,0:T(8,128)(2,1)}, bf16[1,128,2,2048]{1,3,2,0:T(8,128)(2,1)}, u32[]{:S(2)}, u32[]{:S(2)}) collective-permute-start(bf16[1,128,2,2048]{1,3,2,0:T(8,128)(2,1)} %collective-permute-done.2), channel_id=1, source_target_pairs={{0,2},{2,4},{4,6},{6,8},{8,10},{10,12},{12,14},{14,16},{16,18},{18... | collective-permute-start | bytes 3145736 | tf_op jit(solution)/shard_map/ppermute | solution.py:34
  84.5 5.8 %copy-start.4 = (bf16[1,640,1,2048]{1,3,2,0:T(8,128)(2,1)}, bf16[1,640,1,2048]{1,3,2,0:T(8,128)(2,1)S(1)}, u32[]{:S(2)}) copy-start(bf16[1,640,1,2048]{1,3,2,0:T(8,128)(2,1)S(1)} %get-tuple-element.10) | copy-start | bytes 7864324
  90.3 3.3 copy-start.6
  94.5 0.8 copy-start.9
  114.0 277.1 %reduce-scatter.5.cloned.1.call-start = ((), (), s32[]{:S(2)}) async-start(), calls=%async_computation.3 | async-start | bytes 1572864 | tf_op jit(solution)/shard_map/reduce_scatter | solution.py:122
  114.2 92.1 %collective-permute-start.4 = (bf16[1024,2048]{1,0:T(8,128)(2,1)}, bf16[1024,2048]{1,0:T(8,128)(2,1)}, u32[]{:S(2)}, u32[]{:S(2)}) collective-permute-start(bf16[1024,2048]{1,0:T(8,128)(2,1)} %param.7), channel_id=1, source_target_pairs={{0,1},{1,0},{2,3},{3,2},{4,5},{5,4},{6,7},{7,6},{8,9},{9,8},{10,11... | collective-permute-start | bytes 12582920 | tf_op jit(solution)/shard_map/ppermute | solution.py:23
  115.5 102.8 %copy-start.10 = (bf16[16,128,128]{2,1,0:T(8,128)(2,1)S(1)}, bf16[16,128,128]{2,1,0:T(8,128)(2,1)}, u32[]{:S(2)}) copy-start(bf16[16,128,128]{2,1,0:T(8,128)(2,1)} %copy-done.9) | copy-start | bytes 1572868
  115.5 102.9 %copy-start.7 = (bf16[1,640,1,2048]{1,3,2,0:T(8,128)(2,1)S(1)}, bf16[1,640,1,2048]{1,3,2,0:T(8,128)(2,1)}, u32[]{:S(2)}) copy-start(bf16[1,640,1,2048]{1,3,2,0:T(8,128)(2,1)} %get-tuple-element.9) | copy-start | bytes 7864324
  218.3 4.2 %copy-start.12 = (bf16[2048,128]{1,0:T(8,128)(2,1)}, bf16[2048,128]{1,0:T(8,128)(2,1)S(1)}, u32[]{:S(2)}) copy-start(bf16[2048,128]{1,0:T(8,128)(2,1)S(1)} %fusion.10) | copy-start | bytes 1572868
  218.5 5.5 %copy-start.11 = (bf16[1,128,2048]{1,2,0:T(8,128)(2,1)S(1)}, bf16[1,128,2048]{1,2,0:T(8,128)(2,1)}, u32[]{:S(2)}) copy-start(bf16[1,128,2048]{1,2,0:T(8,128)(2,1)} %copy.47) | copy-start | bytes 1572868
  222.5 1.5 copy-start.8
  227.1 6.1 %copy-start.13 = (bf16[2048,128]{1,0:T(8,128)(2,1)S(1)}, bf16[2048,128]{1,0:T(8,128)(2,1)}, u32[]{:S(2)}) copy-start(bf16[2048,128]{1,0:T(8,128)(2,1)} %copy-done.12) | copy-start | bytes 1572868
  233.2 3.8 copy-start.2
  234.2 122.3 %copy-start.3 = (f32[16,128,640]{2,1,0:T(8,128)}, f32[16,128,640]{2,1,0:T(8,128)S(1)}, u32[]{:S(2)}) copy-start(f32[16,128,640]{2,1,0:T(8,128)S(1)} %fusion.37) | copy-start | bytes 15728644
  237.1 28.4 %collective-permute-start.5 = (f32[1,128,2,2048]{1,3,2,0:T(8,128)S(1)}, f32[1,128,2,2048]{1,3,2,0:T(8,128)S(1)}, u32[]{:S(2)}, u32[]{:S(2)}) collective-permute-start(f32[1,128,2,2048]{1,3,2,0:T(8,128)S(1)} %fusion.19), channel_id=1, source_target_pairs={{2,0},{4,2},{6,4},{8,6},{10,8},{12,10},{14,12},{16,14},{18,16},{20... | collective-permute-start | bytes 6291464 | tf_op jit(solution)/shard_map/ppermute | solution.py:34
  265.9 62.0 %collective-permute-start.6 = (f32[1,128,2,2048]{1,3,2,0:T(8,128)S(1)}, f32[1,128,2,2048]{1,3,2,0:T(8,128)S(1)}, u32[]{:S(2)}, u32[]{:S(2)}) collective-permute-start(f32[1,128,2,2048]{1,3,2,0:T(8,128)S(1)} %fusion.21), channel_id=1, source_target_pairs={{2,0},{4,2},{6,4},{8,6},{10,8},{12,10},{14,12},{16,14},{18,16},{20... | collective-permute-start | bytes 6291464 | tf_op jit(solution)/shard_map/ppermute | solution.py:34
  328.0 32.1 %copy-start.5 = (bf16[1,640,1,2048]{1,3,2,0:T(8,128)(2,1)S(1)}, bf16[1,640,1,2048]{1,3,2,0:T(8,128)(2,1)}, u32[]{:S(2)}) copy-start(bf16[1,640,1,2048]{1,3,2,0:T(8,128)(2,1)} %copy-done.4) | copy-start | bytes 7864324
  328.0 28.5 %collective-permute-start.7 = (f32[1,128,2,2048]{1,3,2,0:T(8,128)S(1)}, f32[1,128,2,2048]{1,3,2,0:T(8,128)S(1)}, u32[]{:S(2)}, u32[]{:S(2)}) collective-permute-start(f32[1,128,2,2048]{1,3,2,0:T(8,128)S(1)} %fusion.15), channel_id=1, source_target_pairs={{2,0},{4,2},{6,4},{8,6},{10,8},{12,10},{14,12},{16,14},{18,16},{20... | collective-permute-start | bytes 6291464 | tf_op jit(solution)/shard_map/ppermute | solution.py:34
  358.1 28.6 %collective-permute-start.8 = (f32[1,128,2,2048]{1,3,2,0:T(8,128)}, f32[1,128,2,2048]{1,3,2,0:T(8,128)}, u32[]{:S(2)}, u32[]{:S(2)}) collective-permute-start(f32[1,128,2,2048]{1,3,2,0:T(8,128)} %fusion.22), channel_id=1, source_target_pairs={{2,0},{4,2},{6,4},{8,6},{10,8},{12,10},{14,12},{16,14},{18,16},{20... | collective-permute-start | bytes 6291464 | tf_op jit(solution)/shard_map/ppermute | solution.py:34
  363.5 27.6 %copy-start.1 = (bf16[1,128,2048]{2,1,0:T(8,128)(2,1)S(1)}, bf16[1,128,2048]{2,1,0:T(8,128)(2,1)}, u32[]{:S(2)}) copy-start(bf16[1,128,2048]{2,1,0:T(8,128)(2,1)} %param.6) | copy-start | bytes 1572868
Sparse Core Ops, SparseCore 0:
  114.1 200.3 reduce-scatter.2
  360.2 19.8 reduce-scatter.4
